TPU v7x, 32 devices: a whole 2x2x4 slice. The times are simulated.
32 devices in a mesh: tp: 8 (over y, x, core), dp: 4 (over z).
Axes of the slice: x: 2, y: 2, z: 4, core: 2. Of those that a mesh axis runs over, the one named last changes fastest.
Arguments:
- activations: bfloat16 [64, 512, 4096], P('dp', None, 'tp'), may hold values from -6 to 6
- query_output_cotangent: bfloat16 [64, 512, 4096], P('dp', None, 'tp'), may hold values from -6 to 6
- value_output_cotangent: bfloat16 [64, 512, 4096], P('dp', None, 'tp'), may hold values from -6 to 6
- lengths: int32 [64], P('dp'), may hold values from 1 to 512
- reducing_matrices_pair: bfloat16 [2, 4096, 128], P(None, 'tp'), may hold values from -0.09375 to 0.09375
- expanding_matrices_pair: bfloat16 [2, 128, 4096], P(None, None, 'tp'), may hold values from -0.5 to 0.5
- width_side_projections: bfloat16 [2, 4096, 128], P(None, 'tp'), may hold values from -0.09375 to 0.09375
- narrow_random_sketch: bfloat16 [128, 16], replicated, may hold values from -0.5 to 0.5
- projected_first_moment: float32 [8192], replicated, may hold values from -6 to 6
- projected_second_moment: float32 [8192], replicated, may hold values from 0.1 to 10
- targets: bfloat16 [1024, 8192], P('dp', 'tp'), may hold values from -6 to 6
Outputs:
- scores: float32 [64, 1024], P('dp', 'tp')
All inputs are finite; a program needn't handle non-finite values.
Results may differ from a plain program's by a relative error of at most 0.023.
Values may be sent and summed in bfloat16 or wider, within the bound.
A program may use at most 128 MiB of HBM per device.

v0:
```python
import math
import jax
import jax.numpy as jnp
from jax import lax
from jax.sharding import PartitionSpec as P


def adam_update(features, first_moment, second_moment):
    mixed = 0.9 * first_moment + 0.1 * features
    spread = 0.999 * second_moment + 0.001 * features * features
    return mixed / (jnp.sqrt(spread) + 1e-08)


def combine_factors(reducing_matrices_pair, expanding_matrices_pair, narrow_random_sketch):
    attention_key_reducer = jnp.dot(
        reducing_matrices_pair[0], narrow_random_sketch, preferred_element_type=jnp.float32
    ).astype(jnp.bfloat16)
    value_down_factor = jnp.dot(
        reducing_matrices_pair[1], narrow_random_sketch, preferred_element_type=jnp.float32
    ).astype(jnp.bfloat16)
    query_up_factor = jnp.dot(
        expanding_matrices_pair[0].T, narrow_random_sketch, preferred_element_type=jnp.float32
    ).astype(jnp.bfloat16)
    value_up_factor = jnp.dot(
        expanding_matrices_pair[1].T, narrow_random_sketch, preferred_element_type=jnp.float32
    ).astype(jnp.bfloat16)
    return (attention_key_reducer, value_down_factor, query_up_factor, value_up_factor)


def body(
    activations,
    query_output_cotangent,
    value_output_cotangent,
    lengths,
    reducing_matrices_pair,
    expanding_matrices_pair,
    width_side_projections,
    narrow_random_sketch,
    projected_first_moment,
    projected_second_moment,
    targets,
):
    attention_key_reducer, value_down_factor, query_up_factor, value_up_factor = combine_factors(
        reducing_matrices_pair, expanding_matrices_pair, narrow_random_sketch
    )
    rank_cols = narrow_random_sketch.shape[1]
    w_left = jnp.concatenate(
        [attention_key_reducer, value_down_factor, width_side_projections[0]], axis=1
    )
    w_query = jnp.concatenate([query_up_factor, width_side_projections[1]], axis=1)
    w_value = jnp.concatenate([value_up_factor, width_side_projections[1]], axis=1)
    groups = lax.axis_size("tp")
    parts = lax.axis_size("dp")
    member = lax.axis_index("tp")
    local_ex, seq_len = activations.shape[:2]
    feature_count = projected_first_moment.shape[0]
    positions = jnp.arange(seq_len, dtype=jnp.int32)
    token_mask = (positions[None, :] < lengths[:, None])[..., None]

    def project(rows, weights):
        out = jnp.einsum("esd,dc->esc", rows, weights, preferred_element_type=jnp.float32)
        return out.astype(jnp.bfloat16)

    left = project(activations, w_left)
    right_q = project(query_output_cotangent, w_query)
    right_v = project(value_output_cotangent, w_value)
    narrow = jnp.concatenate(
        [left[..., : 2 * rank_cols], right_q[..., :rank_cols], right_v[..., :rank_cols]], axis=-1
    )
    narrow = jnp.where(token_mask, narrow, jnp.zeros((), jnp.bfloat16))
    narrow = lax.psum(narrow, "tp")

    def outer_sum(first, wide):
        return jnp.einsum(
            "esr,esk->erk",
            narrow[..., first * rank_cols : (first + 1) * rank_cols],
            wide,
            preferred_element_type=jnp.float32,
        )

    own_features = jnp.concatenate(
        [
            outer_sum(2, left[..., 2 * rank_cols :]),
            outer_sum(3, left[..., 2 * rank_cols :]),
            outer_sum(0, right_q[..., rank_cols:]),
            outer_sum(1, right_v[..., rank_cols:]),
        ],
        axis=1,
    ).reshape(local_ex, -1)
    features = lax.psum_scatter(
        own_features.astype(jnp.bfloat16), "tp", scatter_dimension=1, tiled=True
    ).astype(jnp.float32)
    span = feature_count // groups
    first_moment = lax.dynamic_slice_in_dim(projected_first_moment, member * span, span)
    second_moment = lax.dynamic_slice_in_dim(projected_second_moment, member * span, span)
    update = adam_update(features, first_moment, second_moment).astype(jnp.bfloat16)
    update = lax.all_gather(update, "dp", axis=0, tiled=True)
    wide_update = update.astype(jnp.float32)
    target_float = targets.astype(jnp.float32)
    update_sq = jnp.sum(wide_update * wide_update, axis=1)
    target_sq = jnp.sum(target_float * target_float, axis=1)
    dots = lax.dot_general(
        update, targets, (((1,), (1,)), ((), ())), preferred_element_type=jnp.float32
    )
    rows = jnp.concatenate(
        [dots, jnp.broadcast_to(update_sq[:, None], (dots.shape[0], 128))], axis=1
    ).reshape(parts, local_ex, -1)
    extra = jnp.pad(target_sq, (0, 128))
    rows = jnp.concatenate([rows, jnp.broadcast_to(extra, (parts, 8, extra.shape[0]))], axis=1)
    rows = lax.psum(rows, "tp")
    rows = lax.all_to_all(rows, "dp", split_axis=0, concat_axis=0, tiled=True)
    owned = targets.shape[0]
    totals = jnp.moveaxis(rows[:, :, :owned], 0, 1).reshape(local_ex + 8, parts * owned)
    columns = parts * owned // groups
    totals = lax.dynamic_slice_in_dim(totals, member * columns, columns, 1)
    row_scale = lax.rsqrt(rows[0, :local_ex, owned : owned + 1] + 1e-06)
    column_scale = lax.rsqrt(totals[local_ex : local_ex + 1] + 1e-06)
    return totals[:local_ex] * row_scale * column_scale * math.sqrt(feature_count)


def solution(mesh):
    placed = (
        P("dp", None, "tp"),
        P("dp", None, "tp"),
        P("dp", None, "tp"),
        P("dp"),
        P(None, "tp", None),
        P(None, None, "tp"),
        P(None, "tp", None),
        P(),
        P(),
        P(),
        P("dp", "tp"),
    )
    return jax.shard_map(body, mesh=mesh, in_specs=placed, out_specs=P("dp", "tp"), check_vma=False)
```

profile of v0, /device:TPU:0, one launch (start us, length us, event | category | flops | bytes accessed | tf_op | source)
XLA Modules:
  0.0 220.2 jit_solution(16352123582546980845)
XLA Ops:
  6.5 0.0 copy-start
  6.5 0.7 copy-done
  7.2 1.0 convolution_convert_fusion.2
  8.3 1.1 convolution_convert_fusion.3
  9.3 1.0 convolution_convert_fusion.1
  10.4 1.0 convolution_convert_fusion
  11.4 1.0 fusion.55
  12.4 0.1 copy.37
  12.5 6.3 %convert_bitcast_fusion = bf16[16,512,160]{1,2,0:T(8,128)(2,1)S(1)} fusion(bf16[16,512,512]{2,1,0:T(8,128)(2,1)} %param.11, bf16[512,128]{0,1:T(8,128)(2,1)S(1)} %bitcast.53, bf16[512,16]{0,1:T(8,128)(2,1)S(1)} %convolution_convert_fusion.2, bf16[512,16]{0,1:T(8,128)(2,1)S(1)} %convolution_convert_fusion.3), kind=kOutput, calls=%fused_computation | convolution fusion | flops 1343979520 | bytes 11173888 | tf_op jit(solution)/shard_map/esd,dc->esc/dot_general | solution.py:61
  18.8 0.0 copy-start.1
  18.8 0.1 copy.38
  18.9 7.1 %convert_bitcast_fusion.2 = bf16[16,512,144]{1,2,0:T(8,128)(2,1)S(1)} fusion(bf16[16,512,512]{2,1,0:T(8,128)(2,1)} %param.12, bf16[512,16]{0,1:T(8,128)(2,1)S(1)} %convolution_convert_fusion.1, bf16[512,128]{0,1:T(8,128)(2,1)S(1)} %bitcast.49), kind=kOutput, calls=%fused_computation.2 | convolution fusion | flops 1209434112 | bytes 10895360 | tf_op jit(solution)/shard_map/esd,dc->esc/dot_general | solution.py:61
  26.1 0.0 copy-start.8
  26.1 0.0 slice-start
  26.1 7.1 %convert_bitcast_fusion.1 = bf16[16,512,144]{1,2,0:T(8,128)(2,1)S(1)} fusion(bf16[16,512,512]{2,1,0:T(8,128)(2,1)} %param.13, bf16[512,16]{0,1:T(8,128)(2,1)S(1)} %convolution_convert_fusion, bf16[512,128]{0,1:T(8,128)(2,1)S(1)} %bitcast.50), kind=kOutput, calls=%fused_computation.1 | convolution fusion | flops 1209434112 | bytes 10895360 | tf_op jit(solution)/shard_map/esd,dc->esc/dot_general | solution.py:61
  33.2 0.0 copy-done.3
  33.2 0.0 copy-start.5
  33.2 0.0 copy-start.2
  33.2 1.4 copy-done.5
  34.6 0.1 iota_compare_fusion
  34.7 1.3 maximum_select_fusion
  36.0 0.0 all-reduce.4.cloned.1.call-update
  36.0 0.0 reduce-scatter.2.cloned.1.call-start
  36.1 59.4 %all-reduce.4.cloned.1.call-done = bf16[16,512,64]{1,2,0:T(8,128)(2,1)} async-done(((bf16[16,512,64]{1,2,0:T(8,128)(2,1)}), bf16[16,512,64]{1,2,0:T(8,128)(2,1)}) %all-reduce.4.cloned.1.call-update) | async-done | bytes 1048592 | tf_op jit(solution)/shard_map/psum | solution.py:71
  95.5 1.7 fusion.8
  97.2 1.8 fusion.11
  99.0 0.0 copy-done.9
  99.0 0.0 copy-start.7
  99.0 0.6 fusion.14
  99.7 0.7 fusion.17
  100.4 0.9 copy.42
  101.2 0.0 reduce-scatter.2.cloned.1.call-update
  101.3 0.0 all-reduce.6.cloned.1.call-start
  101.3 0.2 multiply_reduce_fusion
  101.5 0.7 dynamic-slice_multiply_fusion.1
  102.2 31.9 %reduce-scatter.2.cloned.1.call-done = bf16[16,1024]{1,0:T(8,128)(2,1)} async-done(((bf16[16,8192]{1,0:T(8,128)(2,1)}), bf16[16,1024]{1,0:T(8,128)(2,1)}) %reduce-scatter.2.cloned.1.call-update) | async-done | bytes 32784 | tf_op jit(solution)/shard_map/reduce_scatter | solution.py:90
  134.1 0.8 fusion.42
  134.9 13.5 %all_gather.3 = bf16[64,1024]{1,0:T(8,128)(2,1)S(1)} all-gather(bf16[16,1024]{1,0:T(8,128)(2,1)S(1)} %fusion.42), channel_id=1, replica_groups=mesh['tp'=8,'dp'=4] {'dp'}, dimensions={0}, use_global_device_ids=true | all-gather | bytes 163840 | tf_op jit(solution)/shard_map/all_gather | solution.py:97
  148.4 0.3 fusion.56
  148.7 0.1 multiply_reduce_fusion.1
  148.8 0.1 broadcast_in_dim.28
  148.9 0.7 pad_maximum_fusion.1
  149.6 0.0 all-reduce.6.cloned.1.call-update
  149.6 52.0 %all-reduce.6.cloned.1.call-done = f32[4,24,384]{2,1,0:T(8,128)} async-done(((f32[4,24,384]{2,1,0:T(8,128)}), f32[4,24,384]{2,1,0:T(8,128)}) %all-reduce.6.cloned.1.call-update) | async-done | bytes 147472 | tf_op jit(solution)/shard_map/psum | solution.py:110
  201.6 4.6 %all-to-all-start = ((f32[4,24,384]{2,1,0:T(8,128)}), f32[4,24,384]{2,1,0:T(8,128)S(1)}, u32[]{:S(2)}, u32[]{:S(2)}) async-start(f32[4,24,384]{2,1,0:T(8,128)} %all-reduce.6.cloned.1.call-done), calls=%async_computation.1 | async-start | bytes 294912 | tf_op jit(solution)/shard_map/all_to_all | solution.py:111
  206.2 6.6 %all-to-all-done = f32[4,24,384]{2,1,0:T(8,128)S(1)} async-done(((f32[4,24,384]{2,1,0:T(8,128)}), f32[4,24,384]{2,1,0:T(8,128)S(1)}, u32[]{:S(2)}, u32[]{:S(2)}) %all-to-all-start) | async-done | bytes 147488 | tf_op jit(solution)/shard_map/all_to_all | solution.py:111
  212.9 0.1 fusion.47
  213.0 0.7 fusion.49
  (21 shorter events, 0.2 us)
Async XLA Ops:
  6.5 0.7 copy-start
  6.5 88.9 %all-reduce.4.cloned.1.call-start = ((), (), s32[]{:S(2)}) async-start(), calls=%async_computation.2 | async-start | bytes 2097152 | tf_op jit(solution)/shard_map/psum | solution.py:71
  18.8 7.2 %copy-start.1 = (bf16[16,512,160]{1,2,0:T(8,128)(2,1)}, bf16[16,512,160]{1,2,0:T(8,128)(2,1)S(1)}, u32[]{:S(2)}) copy-start(bf16[16,512,160]{1,2,0:T(8,128)(2,1)S(1)} %convert_bitcast_fusion) | copy-start | bytes 7864324
  26.0 7.2 %copy-start.3 = (bf16[16,512,144]{1,2,0:T(8,128)(2,1)}, bf16[16,512,144]{1,2,0:T(8,128)(2,1)S(1)}, u32[]{:S(2)}) copy-start(bf16[16,512,144]{1,2,0:T(8,128)(2,1)S(1)} %convert_bitcast_fusion.2) | copy-start | bytes 7077892
  26.1 8.6 %copy-start.8 = (s32[16]{0:T(128)S(1)}, s32[16]{0:T(128)}, u32[]{:S(2)}) copy-start(s32[16]{0:T(128)} %param.14) | copy-start | bytes 196
  26.1 8.6 %slice-start = ((bf16[16,512,160]{1,2,0:T(8,128)(2,1)}), bf16[16,512,32]{1,2,0:T(8,128)(2,1)S(1)}, s32[]{:S(2)}) async-start(bf16[16,512,160]{1,2,0:T(8,128)(2,1)} %copy-done.1), calls=%async_computation.5 | async-start | bytes 1048576 | tf_op jit(solution)/shard_map/slice | solution.py:68
  33.2 1.4 copy-start.5
  33.2 62.3 %copy-start.2 = (bf16[16,512,160]{1,2,0:T(8,128)(2,1)S(1)}, bf16[16,512,160]{1,2,0:T(8,128)(2,1)}, u32[]{:S(2)}) copy-start(bf16[16,512,160]{1,2,0:T(8,128)(2,1)} %copy-done.1) | copy-start | bytes 7864324
  36.0 98.1 %reduce-scatter.2.cloned.1.call-start = ((), (), s32[]{:S(2)}) async-start(), calls=%async_computation.3 | async-start | bytes 294912 | tf_op jit(solution)/shard_map/reduce_scatter | solution.py:90
  95.5 3.5 %copy-start.4 = (bf16[16,512,144]{1,2,0:T(8,128)(2,1)S(1)}, bf16[16,512,144]{1,2,0:T(8,128)(2,1)}, u32[]{:S(2)}) copy-start(bf16[16,512,144]{1,2,0:T(8,128)(2,1)} %copy-done.3) | copy-start | bytes 7077892
  95.5 3.5 %copy-start.9 = (bf16[16,512,64]{1,2,0:T(8,128)(2,1)S(1)}, bf16[16,512,64]{1,2,0:T(8,128)(2,1)}, u32[]{:S(2)}) copy-start(bf16[16,512,64]{1,2,0:T(8,128)(2,1)} %all-reduce.4.cloned.1.call-done) | copy-start | bytes 3145732
  97.2 2.4 %copy-start.6 = (bf16[16,512,144]{1,2,0:T(8,128)(2,1)S(1)}, bf16[16,512,144]{1,2,0:T(8,128)(2,1)}, u32[]{:S(2)}) copy-start(bf16[16,512,144]{1,2,0:T(8,128)(2,1)} %copy-done.5) | copy-start | bytes 7077892
  99.0 2.3 %copy-start.7 = (bf16[256,1024]{1,0:T(8,128)(2,1)S(1)}, bf16[256,1024]{1,0:T(8,128)(2,1)}, u32[]{:S(2)}) copy-start(bf16[256,1024]{1,0:T(8,128)(2,1)} %param.21) | copy-start | bytes 1572868
  101.3 100.4 %all-reduce.6.cloned.1.call-start = ((), (), s32[]{:S(2)}) async-start(), calls=%async_computation.4 | async-start | bytes 294912 | tf_op jit(solution)/shard_map/psum | solution.py:110
  201.6 11.2 %all-to-all-start = ((f32[4,24,384]{2,1,0:T(8,128)}), f32[4,24,384]{2,1,0:T(8,128)S(1)}, u32[]{:S(2)}, u32[]{:S(2)}) async-start(f32[4,24,384]{2,1,0:T(8,128)} %all-reduce.6.cloned.1.call-done), calls=%async_computation.1 | async-start | bytes 294912 | tf_op jit(solution)/shard_map/all_to_all | solution.py:111
Sparse Core Ops, SparseCore 0:
  36.1 59.2 all-reduce.3
  101.4 32.6 reduce-scatter.1
  149.8 51.8 all-reduce.5
where the time goes:
time: 221 us; the launch traced here: 220 us
  waiting for transfers between devices  150 us (68%)
  matrix products  29.7 us (13%)
  blocking collectives  13.5 us (6%)
  between operations  13.3 us (6%)
  other arithmetic  4.71 us (2%)
  starting transfers between devices  4.69 us (2%)
  local copies, waits for them, and re-layouts  4.36 us (2%)
    psum x1, waiting for transfers between devices, body(): narrow = lax.psum(narrow, 'tp')  59.4 us
    psum x1, waiting for transfers between devices, body(): rows = lax.psum(rows, 'tp')  52 us
    reduce_scatter x1, waiting for transfers between devices, body(): lax.psum_scatter(own_features.astype(jnp.bfloat16), 'tp', scatter_dimensi...  31.9 us
    dot_general x3, matrix products, project(): jnp.einsum('esd,dc->esc', rows, weights, preferred_element_type=jnp.float32)  20.4 us
    all_gather x1, blocking collectives, body(): update = lax.all_gather(update, 'dp', axis=0, tiled=True)  13.5 us
    all_to_all x1, waiting for transfers between devices, body(): rows = lax.all_to_all(rows, 'dp', split_axis=0, concat_axis=0, tiled=True)  6.65 us
    dot_general x4, matrix products, outer_sum(): jnp.einsum('esr,esk->erk', narrow[..., first * rank_cols:(first + 1) * ra...  4.82 us
    all_to_all x1, starting transfers between devices, body(): rows = lax.all_to_all(rows, 'dp', split_axis=0, concat_axis=0, tiled=True)  4.6 us
  transfers between devices with their start and end apart: 4, of which 4 were waited for; matrix products, arithmetic and copies ran while one was open for 0% of the time, Pallas kernels for 0%

commit v1 on v0

--- a/solution.py
+++ b/solution.py
@@ -1,8 +1,16 @@
+import functools
 import math
 import jax
 import jax.numpy as jnp
 from jax import lax
 from jax.sharding import PartitionSpec as P
+
+
+def _create_group(content, chip_axis):
+    return jax.lax.all_gather(content, chip_axis).sum(axis=0)
+
+
+clear_tiles_in = functools.partial(_create_group, chip_axis="tp")
 
 
 def adam_update(features, first_moment, second_moment):
@@ -107,7 +115,7 @@
     ).reshape(parts, local_ex, -1)
     extra = jnp.pad(target_sq, (0, 128))
     rows = jnp.concatenate([rows, jnp.broadcast_to(extra, (parts, 8, extra.shape[0]))], axis=1)
-    rows = lax.psum(rows, "tp")
+    rows = clear_tiles_in(rows)
     rows = lax.all_to_all(rows, "dp", split_axis=0, concat_axis=0, tiled=True)
     owned = targets.shape[0]
     totals = jnp.moveaxis(rows[:, :, :owned], 0, 1).reshape(local_ex + 8, parts * owned)

time: 221 us -> 195 us (0.88)
  waiting for transfers between devices: 150 us -> 122 us
    psum x1 -> x0, waiting for transfers between devices: 52 us -> none  [body(): rows = lax.psum(rows, 'tp')]
    all_gather x0 -> x1, waiting for transfers between devices: none -> 24.1 us  [_create_group(): return jax.lax.all_gather(content, chip_axis).sum(axis=0)]
where the time goes in v1:
time: 195 us; the launch traced here: 194 us
  waiting for transfers between devices  122 us (63%)
  matrix products  29.7 us (15%)
  blocking collectives  13.5 us (7%)
  between operations  13.3 us (7%)
  other arithmetic  6.71 us (3%)
  starting transfers between devices  4.68 us (2%)
  local copies, waits for them, and re-layouts  4.36 us (2%)
    psum x1, waiting for transfers between devices, body(): narrow = lax.psum(narrow, 'tp')  59.4 us
    reduce_scatter x1, waiting for transfers between devices, body(): lax.psum_scatter(own_features.astype(jnp.bfloat16), 'tp', scatter_dimensi...  31.9 us
    all_gather x1, waiting for transfers between devices, _create_group(): return jax.lax.all_gather(content, chip_axis).sum(axis=0)  24.1 us
    dot_general x3, matrix products, project(): jnp.einsum('esd,dc->esc', rows, weights, preferred_element_type=jnp.float32)  20.4 us
    all_gather x1, blocking collectives, body(): update = lax.all_gather(update, 'dp', axis=0, tiled=True)  13.5 us
    all_to_all x1, waiting for transfers between devices, body(): rows = lax.all_to_all(rows, 'dp', split_axis=0, concat_axis=0, tiled=True)  6.57 us
    dot_general x4, matrix products, outer_sum(): jnp.einsum('esr,esk->erk', narrow[..., first * rank_cols:(first + 1) * ra...  4.83 us
    all_to_all x1, starting transfers between devices, body(): rows = lax.all_to_all(rows, 'dp', split_axis=0, concat_axis=0, tiled=True)  4.6 us
  transfers between devices with their start and end apart: 4, of which 4 were waited for; matrix products, arithmetic and copies ran while one was open for 0% of the time, Pallas kernels for 0%

profile of v1, /device:TPU:0, one launch (start us, length us, event | category | flops | bytes accessed | tf_op | source)
XLA Modules:
  0.0 194.3 jit_solution(7509525870104352613)
XLA Ops:
  6.5 0.7 copy-done
  7.2 1.0 convolution_convert_fusion.2
  8.3 1.1 convolution_convert_fusion.3
  9.3 1.0 convolution_convert_fusion.1
  10.4 1.0 convolution_convert_fusion
  11.4 1.0 fusion.55
  12.4 0.1 copy.36
  12.5 6.3 %convert_bitcast_fusion = bf16[16,512,160]{1,2,0:T(8,128)(2,1)S(1)} fusion(bf16[16,512,512]{2,1,0:T(8,128)(2,1)} %param.11, bf16[512,128]{0,1:T(8,128)(2,1)S(1)} %bitcast.55, bf16[512,16]{0,1:T(8,128)(2,1)S(1)} %convolution_convert_fusion.2, bf16[512,16]{0,1:T(8,128)(2,1)S(1)} %convolution_convert_fusion.3), kind=kOutput, calls=%fused_computation | convolution fusion | flops 1343979520 | bytes 11173888 | tf_op jit(solution)/shard_map/esd,dc->esc/dot_general | solution.py:69
  18.8 0.0 copy-start.1
  18.8 0.1 copy.37
  18.9 7.1 %convert_bitcast_fusion.2 = bf16[16,512,144]{1,2,0:T(8,128)(2,1)S(1)} fusion(bf16[16,512,512]{2,1,0:T(8,128)(2,1)} %param.12, bf16[512,16]{0,1:T(8,128)(2,1)S(1)} %convolution_convert_fusion.1, bf16[512,128]{0,1:T(8,128)(2,1)S(1)} %bitcast.50), kind=kOutput, calls=%fused_computation.2 | convolution fusion | flops 1209434112 | bytes 10895360 | tf_op jit(solution)/shard_map/esd,dc->esc/dot_general | solution.py:69
  26.1 0.0 copy-start.8
  26.1 0.0 slice-start
  26.1 7.1 %convert_bitcast_fusion.1 = bf16[16,512,144]{1,2,0:T(8,128)(2,1)S(1)} fusion(bf16[16,512,512]{2,1,0:T(8,128)(2,1)} %param.13, bf16[512,16]{0,1:T(8,128)(2,1)S(1)} %convolution_convert_fusion, bf16[512,128]{0,1:T(8,128)(2,1)S(1)} %bitcast.51), kind=kOutput, calls=%fused_computation.1 | convolution fusion | flops 1209434112 | bytes 10895360 | tf_op jit(solution)/shard_map/esd,dc->esc/dot_general | solution.py:69
  33.2 0.0 copy-done.3
  33.2 0.0 copy-start.5
  33.2 0.0 copy-start.2
  33.2 1.4 copy-done.5
  34.6 0.1 iota_compare_fusion
  34.7 1.3 maximum_select_fusion
  36.0 0.0 all-reduce.3.cloned.1.call-update
  36.0 0.0 reduce-scatter.2.cloned.1.call-start
  36.1 59.4 %all-reduce.3.cloned.1.call-done = bf16[16,512,64]{1,2,0:T(8,128)(2,1)} async-done(((bf16[16,512,64]{1,2,0:T(8,128)(2,1)}), bf16[16,512,64]{1,2,0:T(8,128)(2,1)}) %all-reduce.3.cloned.1.call-update) | async-done | bytes 1048592 | tf_op jit(solution)/shard_map/psum | solution.py:79
  95.5 1.7 fusion.8
  97.2 1.8 fusion.11
  99.0 0.0 copy-done.9
  99.0 0.7 fusion.14
  99.7 0.0 copy-done.6
  99.7 0.7 fusion.17
  100.4 0.9 copy.41
  101.2 0.0 reduce-scatter.2.cloned.1.call-update
  101.3 0.0 all-gather.3.cloned.1.call-start
  101.3 0.2 multiply_reduce_fusion
  101.5 0.7 dynamic-slice_multiply_fusion.1
  102.2 31.9 %reduce-scatter.2.cloned.1.call-done = bf16[16,1024]{1,0:T(8,128)(2,1)} async-done(((bf16[16,8192]{1,0:T(8,128)(2,1)}), bf16[16,1024]{1,0:T(8,128)(2,1)}) %reduce-scatter.2.cloned.1.call-update) | async-done | bytes 32784 | tf_op jit(solution)/shard_map/reduce_scatter | solution.py:98
  134.1 0.8 fusion.42
  134.9 13.5 %all_gather.9 = bf16[64,1024]{1,0:T(8,128)(2,1)S(1)} all-gather(bf16[16,1024]{1,0:T(8,128)(2,1)S(1)} %fusion.42), channel_id=1, replica_groups=mesh['tp'=8,'dp'=4] {'dp'}, dimensions={0}, use_global_device_ids=true | all-gather | bytes 163840 | tf_op jit(solution)/shard_map/all_gather | solution.py:105
  148.4 0.3 fusion.56
  148.7 0.1 multiply_reduce_fusion.1
  148.8 0.1 broadcast_in_dim.28
  148.9 0.7 pad_maximum_fusion.1
  149.6 0.0 all-gather.3.cloned.1.call-update
  149.6 24.1 %all-gather.3.cloned.1.call-done = f32[32,24,384]{2,1,0:T(8,128)} async-done(((f32[4,24,384]{2,1,0:T(8,128)}), f32[32,24,384]{2,1,0:T(8,128)}) %all-gather.3.cloned.1.call-update) | async-done | bytes 1179664 | tf_op jit(solution)/shard_map/all_gather | solution.py:10
  173.8 2.0 %reduce_sum.29 = f32[4,24,384]{2,1,0:T(8,128)} reduce(f32[8,4,24,384]{3,2,1,0:T(8,128)} %bitcast.52, f32[]{:T(128)} %constant.13.clone.1), dimensions={0}, to_apply=%region_4.5 | reduce | flops 258048 | bytes 1327108 | tf_op jit(solution)/shard_map/reduce_sum | solution.py:10
  175.8 4.6 %all-to-all-start = ((f32[4,24,384]{2,1,0:T(8,128)}), f32[4,24,384]{2,1,0:T(8,128)S(1)}, u32[]{:S(2)}, u32[]{:S(2)}) async-start(f32[4,24,384]{2,1,0:T(8,128)} %reduce_sum.29), calls=%async_computation.1 | async-start | bytes 294912 | tf_op jit(solution)/shard_map/all_to_all | solution.py:119
  180.4 6.6 %all-to-all-done = f32[4,24,384]{2,1,0:T(8,128)S(1)} async-done(((f32[4,24,384]{2,1,0:T(8,128)}), f32[4,24,384]{2,1,0:T(8,128)S(1)}, u32[]{:S(2)}, u32[]{:S(2)}) %all-to-all-start) | async-done | bytes 147488 | tf_op jit(solution)/shard_map/all_to_all | solution.py:119
  187.0 0.1 fusion.47
  187.1 0.7 fusion.49
  (22 shorter events, 0.2 us)
Async XLA Ops:
  6.5 0.7 copy-start
  6.5 88.9 %all-reduce.3.cloned.1.call-start = ((), (), s32[]{:S(2)}) async-start(), calls=%async_computation.2 | async-start | bytes 2097152 | tf_op jit(solution)/shard_map/psum | solution.py:79
  18.8 7.2 %copy-start.1 = (bf16[16,512,160]{1,2,0:T(8,128)(2,1)}, bf16[16,512,160]{1,2,0:T(8,128)(2,1)S(1)}, u32[]{:S(2)}) copy-start(bf16[16,512,160]{1,2,0:T(8,128)(2,1)S(1)} %convert_bitcast_fusion) | copy-start | bytes 7864324
  26.0 7.2 %copy-start.3 = (bf16[16,512,144]{1,2,0:T(8,128)(2,1)}, bf16[16,512,144]{1,2,0:T(8,128)(2,1)S(1)}, u32[]{:S(2)}) copy-start(bf16[16,512,144]{1,2,0:T(8,128)(2,1)S(1)} %convert_bitcast_fusion.2) | copy-start | bytes 7077892
  26.1 8.6 %copy-start.8 = (s32[16]{0:T(128)S(1)}, s32[16]{0:T(128)}, u32[]{:S(2)}) copy-start(s32[16]{0:T(128)} %param.14) | copy-start | bytes 196
  26.1 8.6 %slice-start = ((bf16[16,512,160]{1,2,0:T(8,128)(2,1)}), bf16[16,512,32]{1,2,0:T(8,128)(2,1)S(1)}, s32[]{:S(2)}) async-start(bf16[16,512,160]{1,2,0:T(8,128)(2,1)} %copy-done.1), calls=%async_computation.5 | async-start | bytes 1048576 | tf_op jit(solution)/shard_map/slice | solution.py:76
  33.2 1.4 copy-start.5
  33.2 62.3 %copy-start.2 = (bf16[16,512,160]{1,2,0:T(8,128)(2,1)S(1)}, bf16[16,512,160]{1,2,0:T(8,128)(2,1)}, u32[]{:S(2)}) copy-start(bf16[16,512,160]{1,2,0:T(8,128)(2,1)} %copy-done.1) | copy-start | bytes 7864324
  36.0 98.1 %reduce-scatter.2.cloned.1.call-start = ((), (), s32[]{:S(2)}) async-start(), calls=%async_computation.3 | async-start | bytes 294912 | tf_op jit(solution)/shard_map/reduce_scatter | solution.py:98
  95.5 3.5 %copy-start.4 = (bf16[16,512,144]{1,2,0:T(8,128)(2,1)S(1)}, bf16[16,512,144]{1,2,0:T(8,128)(2,1)}, u32[]{:S(2)}) copy-start(bf16[16,512,144]{1,2,0:T(8,128)(2,1)} %copy-done.3) | copy-start | bytes 7077892
  95.5 3.5 %copy-start.9 = (bf16[16,512,64]{1,2,0:T(8,128)(2,1)S(1)}, bf16[16,512,64]{1,2,0:T(8,128)(2,1)}, u32[]{:S(2)}) copy-start(bf16[16,512,64]{1,2,0:T(8,128)(2,1)} %all-reduce.3.cloned.1.call-done) | copy-start | bytes 3145732
  97.2 2.4 %copy-start.6 = (bf16[16,512,144]{1,2,0:T(8,128)(2,1)S(1)}, bf16[16,512,144]{1,2,0:T(8,128)(2,1)}, u32[]{:S(2)}) copy-start(bf16[16,512,144]{1,2,0:T(8,128)(2,1)} %copy-done.5) | copy-start | bytes 7077892
  99.7 1.7 copy-start.7
  101.3 72.5 %all-gather.3.cloned.1.call-start = ((), (), s32[]{:S(2)}) async-start(), calls=%async_computation.4 | async-start | bytes 1327104 | tf_op jit(solution)/shard_map/all_gather | solution.py:10
  175.8 11.2 %all-to-all-start = ((f32[4,24,384]{2,1,0:T(8,128)}), f32[4,24,384]{2,1,0:T(8,128)S(1)}, u32[]{:S(2)}, u32[]{:S(2)}) async-start(f32[4,24,384]{2,1,0:T(8,128)} %reduce_sum.29), calls=%async_computation.1 | async-start | bytes 294912 | tf_op jit(solution)/shard_map/all_to_all | solution.py:119
Sparse Core Ops, SparseCore 0:
  36.1 59.2 all-reduce.2
  101.4 32.6 reduce-scatter.1
  149.8 23.9 all-gather.2
